TPU v7x, 128 devices: a whole 4x4x4 slice. The times are simulated.
128 devices in a mesh: sec: 2 (over core), tile: 64 (over z, y, x).
Axes of the slice: x: 4, y: 4, z: 4, core: 2. Of those that a mesh axis runs over, the one named last changes fastest.
Arguments:
- adjoint_state: bfloat16 [2, 75, 2359296], P('sec', None, 'tile'), may hold values from -6 to 6
- tangent_coef: bfloat16 [2, 75, 2359296], P('sec', None, 'tile'), may hold values from 0.5 to 1.5
- column_ops: bfloat16 [2, 16, 75, 75], P('sec')
- surf_read: bfloat16 [2, 4, 75], P('sec'), may hold values from -0.75 to 0.75
- surf_write: float32 [2, 75, 4], P('sec'), may hold values from -3 to 3
- remap_weights: bfloat16 [64, 64, 16, 4096], P('tile')
- pair_atmos: int32 [64, 64, 16], P('tile'), may hold values from 0 to 575
- pair_ocean: int32 [64, 64, 16], P('tile'), may hold values from 0 to 36863, as said below
- list_len: int32 [64, 64], P('tile'), may hold values from 0 to 16, as said below
- ocean_owned: int32 [64, 576], P('tile'), may hold values from 0 to 36863, as said below
Outputs:
- adjoint_out: bfloat16 [2, 75, 2359296], P('sec', None, 'tile')
Inputs may be any that keep to these rules, and one draw needn't show every extreme that they name: pair_ocean[t, d, c] is one of the blocks in row d of ocean_owned. Every global ocean block stands exactly once in ocean_owned. Slots c >= list_len[t, d] are empty; in every draw some ocean tile receives a full list of 16 pairs from every atmosphere tile.
All inputs are finite; a program needn't handle non-finite values.
Results may differ from a plain program's by a relative error of at most 0.012.
Values may be sent and summed in bfloat16 or wider, within the bound.
No kernel may reach another device: no remote copies, remote signals or barrier semaphores. Data moves between devices by JAX's collectives and lax.ppermute only.
A program may use at most 128 MiB of HBM per device.

v0:
```python
import jax
import jax.numpy as jnp
from jax import lax
from jax.experimental import pallas as pl
from jax.experimental.pallas import tpu as pltpu
from jax.sharding import PartitionSpec as P

NF = 4
BLK = 64
NSTEP = 16
LANES = 128
GROUP = 8
MANY = 2
WIDTH = 4096
FIRST = 2
BF16 = jnp.bfloat16
F32 = jnp.float32


def lanes_below(shape, edge):
    return lax.broadcasted_iota(jnp.int32, shape, len(shape) - 1) < edge


def advance(ops_ref, current, coef):
    factors = coef.astype(F32)
    for step in range(NSTEP):
        stepped = lax.dot_general(
            ops_ref[step], current, (((0,), (0,)), ((), ())), preferred_element_type=F32
        )
        current = (stepped * factors).astype(BF16)
    return current


def early_column(block):
    return block // 2 * 3 + block % 2


def surface_kernel(
    read_ref, ops_ref, state_hbm, coef_hbm, out_ref, swept_hbm, state, coef, swept, held, sems
):
    count = coef.shape[0]
    parts = sems.shape[0] - 2 * count
    tiles = WIDTH // LANES

    def columns(part):
        return pl.ds(pl.multiple_of(part * WIDTH, WIDTH), WIDTH)

    def fetch(part):
        return pltpu.make_async_copy(
            state_hbm.at[:, columns(part)], state.at[:, columns(part)], sems.at[part]
        )

    def fetch_coef(block):
        return pltpu.make_async_copy(
            coef_hbm.at[:, columns(early_column(block))], coef.at[block], sems.at[parts + block]
        )

    def store(block):
        return pltpu.make_async_copy(
            swept.at[block], swept_hbm.at[:, columns(block)], sems.at[parts + count + block]
        )

    ahead = [early_column(block) for block in range(count)]
    for block in range(count):
        fetch(ahead[block]).start()
        fetch_coef(block).start()
    for part in range(parts):
        if part not in ahead:
            fetch(part).start()

    def sweep_block(block, carry):
        part = early_column(block)
        fetch(part).wait()
        fetch_coef(block).wait()
        swept[block] = advance(ops_ref, state[:, columns(part)], coef[block])
        store(block).start()
        return carry

    lax.fori_loop(0, count, sweep_block, 0)
    for part in range(parts):
        if part not in ahead:
            fetch(part).wait()

    def compute(part, carry):
        fields = jnp.dot(read_ref[...], state[:, columns(part)], preferred_element_type=F32)
        for tile in range(tiles):
            row = pl.multiple_of((part * tiles + tile) * 8, 8)
            held[pl.ds(row, NF), :] = fields[:, tile * LANES : (tile + 1) * LANES]
        return carry

    lax.fori_loop(0, parts, compute, 0)
    pairs = out_ref.shape[0] // 2
    left = lanes_below((pairs, LANES), BLK)
    for duo in range(NF // 2):
        first = held[pl.ds(2 * duo, pairs, stride=8), :]
        second = held[pl.ds(2 * duo + 1, pairs, stride=8), :]
        cols = slice(duo * LANES, (duo + 1) * LANES)
        even = jnp.where(left, first, pltpu.roll(second, BLK, 1))
        odd = jnp.where(left, pltpu.roll(first, BLK, 1), second)
        out_ref[:pairs, cols] = even.astype(BF16)
        out_ref[pairs:, cols] = odd.astype(BF16)
    for block in range(count):
        store(block).wait()


def surface_blocks(read, ops, state, coef):
    levels, cells = state.shape
    blocks = cells // BLK
    parts = cells // WIDTH
    whole = pl.BlockSpec(memory_space=pltpu.VMEM)
    there = pl.BlockSpec(memory_space=pl.ANY)
    return pl.pallas_call(
        surface_kernel,
        out_shape=(
            jax.ShapeDtypeStruct((blocks, NF * BLK), BF16),
            pltpu.HBM((levels, cells // 3 * 2), BF16),
        ),
        in_specs=[whole, whole, there, there],
        out_specs=(whole, there),
        scratch_shapes=[
            pltpu.VMEM((levels, cells), BF16),
            pltpu.VMEM((FIRST, levels, WIDTH), BF16),
            pltpu.VMEM((FIRST, levels, WIDTH), BF16),
            pltpu.VMEM((blocks // 2 * 8, LANES), F32),
            pltpu.SemaphoreType.DMA((parts + 2 * FIRST,)),
        ],
        compiler_params=pltpu.CompilerParams(vmem_limit_bytes=28 << 20),
        name="surface",
    )(read, ops, state, coef)


def fetch_weights(weights_hbm, weights, sems, part):
    lists = pl.ds(part * GROUP, GROUP)
    return pltpu.make_async_copy(weights_hbm.at[lists], weights.at[lists], sems.at[part])


def half_list(weights, tile, half):
    return jnp.concatenate(
        [weights[tile, half, :, q * LANES : (q + 1) * LANES] for q in range(BLK // 2)], 0
    )


def fill_spread(spread):
    row = lax.broadcasted_iota(jnp.int32, spread.shape, 0)
    col = lax.broadcasted_iota(jnp.int32, spread.shape, 1)
    source = (col >> 9) * BLK + ((col >> 3) & 31) * 2 + ((col >> 8) & 1)
    spread[...] = jnp.where(row == source, 1.0, 0.0).astype(BF16)


def own_slot(rows, cols):
    row = lax.broadcasted_iota(jnp.int32, (rows, cols), 0)
    col = lax.broadcasted_iota(jnp.int32, (rows, cols), 1)
    return (row & 7) == (col & 7)


def pick(values, lanes):
    return jnp.take_along_axis(values, lanes, axis=1, mode="promise_in_bounds")


def widened(values):
    rows, cols = values.shape
    return jnp.concatenate([values, jnp.zeros((rows, LANES - cols), values.dtype)], 1)


def slot_rows(values):
    lists = values.shape[0]
    lane = lax.broadcasted_iota(jnp.int32, (lists, LANES), 1)
    row = lax.broadcasted_iota(jnp.int32, (lists, LANES), 0)
    spread = jnp.where((lane >> 4) == (row & 7), pick(widened(values), lane & 15), 0.0)
    return jnp.sum(spread.reshape(lists // 8, 8, LANES), 1)


def even_first(values, padded):
    count = values.shape[1]
    pairs = count // 2
    lane = lax.broadcasted_iota(jnp.int32, (8, LANES), 1)
    sources = []
    for start in range(0, count, LANES):
        source = values[:, start : min(start + LANES, count)]
        sources.append(source if source.shape[1] == LANES else widened(source))
    sources = [jnp.broadcast_to(source, (8, LANES)) for source in sources]
    tiles = []
    for tile in range(padded // LANES):
        spots = [
            2 * j if j < pairs else 2 * (j - pairs) + 1
            for j in range(tile * LANES, min((tile + 1) * LANES, count))
        ]
        at = tile * LANES + lane
        wanted = jnp.where(at < pairs, 2 * at, 2 * (at - pairs) + 1)
        result = jnp.full((8, LANES), -2.0, F32)
        for index in sorted({spot // LANES for spot in spots}):
            inside = ((wanted >> 7) == index) & (at < count)
            result = jnp.where(inside, pick(sources[index], wanted & 127), result)
        tiles.append(result)
    return jnp.concatenate(tiles, 1)[:1]


def outgoing_kernel(
    section_ref,
    atmos_ref,
    length_ref,
    ids_ref,
    owned_ref,
    blocks_ref,
    weights_hbm,
    out_ref,
    in_key_ref,
    in_table_ref,
    chosen,
    spread,
    wide,
    weights,
    weight_sems,
):
    @pl.when(section_ref[0] == 1)
    def _():
        for part in range(weight_sems.shape[0]):
            fetch_weights(weights_hbm, weights, weight_sems, part).start()

    blocks = blocks_ref.shape[0]
    pairs = blocks // 2
    padded = in_table_ref.shape[1]
    parts = in_key_ref.shape[0]
    first = section_ref[0] == 0
    lane = lax.broadcasted_iota(jnp.int32, (8, LANES), 1)
    row = lax.broadcasted_iota(jnp.int32, (8, LANES), 0)
    lengths = jnp.broadcast_to(widened(length_ref[...].astype(F32)), (8, LANES))
    live = (lane & 15).astype(F32) < pick(lengths, row * 8 + (lane >> 4))
    atmos = atmos_ref[...]
    atmos = ((atmos & 1) * pairs + (atmos >> 1)).astype(F32)
    atmos_key = jnp.where(live, slot_rows(widened(atmos).T[: atmos.shape[1]]), -1.0)
    ocean_key = slot_rows(ids_ref[:, 0, :].astype(F32))
    owned_table = even_first(owned_ref[...].astype(F32), padded)
    plain_table = lax.broadcasted_iota(jnp.int32, (1, padded), 1).astype(F32)
    out_key = jnp.where(first, ocean_key, atmos_key)
    out_table = jnp.where(first, owned_table, plain_table)
    in_key_ref[...] = jnp.where(first, atmos_key, ocean_key)
    in_table_ref[...] = jnp.where(first, plain_table, owned_table)

    for part in range(parts):
        key = jnp.broadcast_to(out_key[part : part + 1, :], (LANES, LANES)).T
        pieces = []
        for start in range(0, blocks, LANES):
            stop = min(start + LANES, blocks)
            piece = jnp.where(key == out_table[:, start : start + LANES], 1.0, 0.0).astype(BF16)
            pieces.append(piece[:, : stop - start])
        chosen[part * LANES : (part + 1) * LANES, :] = jnp.dot(
            jnp.concatenate(pieces, 1), blocks_ref[...], preferred_element_type=F32
        )

    @pl.when(first)
    def _():
        out_ref[...] = chosen[...].astype(BF16)

    @pl.when(jnp.logical_not(first))
    def _():
        fill_spread(spread)
        left = lane < BLK
        mine = own_slot(MANY * LANES, 2 * LANES)

        def lists(part, carry):
            span = MANY * LANES
            here = pl.ds(pl.multiple_of(part * span, span), span)
            for duo in range(NF // 2):
                values = chosen[here, duo * LANES : (duo + 1) * LANES].astype(BF16)
                for chunk in range(4):
                    cols = slice(chunk * 2 * LANES, (chunk + 1) * 2 * LANES)
                    spaced = jnp.dot(values, spread[:, cols], preferred_element_type=F32)
                    wide[:, (duo * 4 + chunk) * 2 * LANES : (duo * 4 + chunk + 1) * 2 * LANES] = (
                        jnp.where(mine, spaced, 0.0)
                    )
            for piece in range(MANY):
                fetch_weights(weights_hbm, weights, weight_sems, part * MANY + piece).wait()
            for inner in range(MANY * GROUP):
                tile = part * MANY * GROUP + inner
                rows = pl.ds(pl.multiple_of(tile * 16, 16), 16)
                results = []
                for half in range(2):
                    start = inner * 16 + half * 8
                    lines = [
                        wide[start : start + 8, line * 2 * LANES : (line + 1) * 2 * LANES]
                        for line in range(2 * NF)
                    ]
                    product = jnp.dot(
                        jnp.concatenate(lines, 0).astype(BF16),
                        half_list(weights, tile, half),
                        preferred_element_type=F32,
                    )
                    sums = []
                    for field in range(NF):
                        even = product[field * 16 : field * 16 + 8]
                        odd = product[field * 16 + 8 : field * 16 + 16]
                        total = jnp.where(left, even, odd)
                        sums.append(total + pltpu.roll(total, BLK, 1))
                    results.append(
                        [jnp.where(left, sums[2 * duo], sums[2 * duo + 1]) for duo in range(NF // 2)]
                    )
                for duo in range(NF // 2):
                    out_ref[rows, duo * LANES : (duo + 1) * LANES] = jnp.concatenate(
                        [results[0][duo], results[1][duo]], 0
                    ).astype(BF16)
            return carry

        lax.fori_loop(0, parts // MANY, lists, 0)


def outgoing(section, atmos, length, ids, owned, blocks, weights):
    lists, halves, cap, _ = weights.shape
    slots = lists * halves * cap
    count, width = blocks.shape
    padded = -(-count // LANES) * LANES
    whole = pl.BlockSpec(memory_space=pltpu.VMEM)
    there = pl.BlockSpec(memory_space=pl.ANY)
    return pl.pallas_call(
        outgoing_kernel,
        out_shape=(
            jax.ShapeDtypeStruct((slots, width), BF16),
            jax.ShapeDtypeStruct((slots // LANES, LANES), F32),
            jax.ShapeDtypeStruct((1, padded), F32),
        ),
        in_specs=[pl.BlockSpec(memory_space=pltpu.SMEM)] + [whole] * 5 + [there],
        out_specs=(whole,) * 3,
        scratch_shapes=[
            pltpu.VMEM((slots, width), F32),
            pltpu.VMEM((LANES, 8 * LANES), BF16),
            pltpu.VMEM((MANY * LANES, 16 * LANES), F32),
            pltpu.VMEM(weights.shape, BF16),
            pltpu.SemaphoreType.DMA((lists // GROUP,)),
        ],
        compiler_params=pltpu.CompilerParams(vmem_limit_bytes=32 << 20),
        name="outgoing",
    )(section, atmos, length, ids, owned, blocks, weights)


def early_kernel(ops_ref, state_ref, coef_ref, swept_hbm, out_ref):
    out_ref[...] = advance(ops_ref, state_ref[...], coef_ref[...])


def early_sweep(ops, state, coef, swept, start, stop):
    levels, _ = state.shape
    columns = pl.BlockSpec((levels, WIDTH), lambda i: (0, early_column(i + start)))
    there = pl.BlockSpec(memory_space=pl.ANY)
    return pl.pallas_call(
        early_kernel,
        grid=(stop - start,),
        out_shape=pltpu.HBM(swept.shape, BF16),
        in_specs=[pl.BlockSpec(ops.shape, lambda i: (0, 0, 0)), columns, columns, there],
        out_specs=pl.BlockSpec((levels, WIDTH), lambda i: (0, i + start)),
        input_output_aliases={3: 0},
        compiler_params=pltpu.CompilerParams(vmem_limit_bytes=16 << 20),
        name="early",
    )(ops, state, coef, swept)


def backward_lists(arrived_ref, weights_hbm, weights, terms, spread, wide, weight_sems):
    left = lanes_below((8, LANES), BLK)
    mine = own_slot(8, 2 * LANES)
    fill_spread(spread)

    def lists(part, carry):
        for piece in range(MANY):
            fetch_weights(weights_hbm, weights, weight_sems, part * MANY + piece).wait()
        for inner in range(MANY * GROUP):
            tile = part * MANY * GROUP + inner
            echoes = arrived_ref[pl.ds(pl.multiple_of(tile * 16, 16), 16), :].astype(F32)
            for half in range(2):
                lines = []
                for duo in range(NF // 2):
                    both = echoes[half * 8 : half * 8 + 8, duo * LANES : (duo + 1) * LANES]
                    turned = pltpu.roll(both, BLK, 1)
                    lines += [
                        jnp.where(left, both, 0.0),
                        jnp.where(left, 0.0, turned),
                        jnp.where(left, turned, 0.0),
                        jnp.where(left, 0.0, both),
                    ]
                product = lax.dot_general(
                    jnp.concatenate(lines, 0).astype(BF16),
                    half_list(weights, tile, half),
                    (((1,), (1,)), ((), ())),
                    preferred_element_type=F32,
                )
                start = inner * 16 + half * 8
                for line in range(2 * NF):
                    wide[start : start + 8, line * 2 * LANES : (line + 1) * 2 * LANES] = jnp.where(
                        mine, product[line * 8 : line * 8 + 8], 0.0
                    )
        span = MANY * LANES
        here = pl.ds(pl.multiple_of(part * span, span), span)
        for duo in range(NF // 2):
            terms[here, duo * LANES : (duo + 1) * LANES] = lax.dot_general(
                wide[:, duo * 8 * LANES : (duo + 1) * 8 * LANES].astype(BF16),
                spread[...],
                (((1,), (1,)), ((), ())),
                preferred_element_type=F32,
            ).astype(BF16)
        return carry

    lax.fori_loop(0, weights.shape[0] // GROUP // MANY, lists, 0)


def sum_terms(key_ref, table_ref, terms, forcing):
    slots = terms.shape[0]
    pairs = forcing.shape[0] // 8
    table = jnp.broadcast_to(table_ref[...], (LANES, table_ref.shape[1])).T[: 2 * pairs]
    picks = [
        jnp.where(table == key_ref[r : r + 1, :], 1.0, 0.0).astype(BF16)
        for r in range(slots // LANES)
    ]
    total = jnp.dot(jnp.concatenate(picks, 1), terms[...], preferred_element_type=F32)
    left = lanes_below((pairs, LANES), BLK)
    for duo in range(NF // 2):
        even = total[:pairs, duo * LANES : (duo + 1) * LANES]
        odd = total[pairs:, duo * LANES : (duo + 1) * LANES]
        fields = (
            jnp.where(left, even, pltpu.roll(odd, BLK, 1)),
            jnp.where(left, pltpu.roll(even, BLK, 1), odd),
        )
        for n, field in enumerate(fields):
            coarse = field.astype(BF16).astype(F32)
            forcing[pl.ds(2 * duo + n, pairs, stride=8), :] = coarse
            forcing[pl.ds(NF + 2 * duo + n, pairs, stride=8), :] = field - coarse


def late_kernel(
    section_ref,
    key_ref,
    table_ref,
    arrived_hbm,
    weights_hbm,
    write_ref,
    ops_ref,
    swept_hbm,
    state_ref,
    coef_ref,
    out_hbm,
    arrived,
    terms,
    forcing,
    early,
    last,
    spread,
    wide,
    weights,
    weight_sems,
    sems,
):
    step = pl.program_id(0)
    backward = jnp.logical_and(step == 0, section_ref[0] == 0)
    slot = step % 2
    before = 1 - slot
    arrival = pltpu.make_async_copy(arrived_hbm, arrived, sems.at[6])

    def fetch(block, into):
        columns = pl.ds(pl.multiple_of(block * 2 * WIDTH, 2 * WIDTH), 2 * WIDTH)
        return pltpu.make_async_copy(swept_hbm.at[:, columns], early.at[into], sems.at[4 + into])

    @pl.when(step == 0)
    def _():
        arrival.start()
        fetch(step, slot).start()

    @pl.when(backward)
    def _():
        for part in range(weight_sems.shape[0]):
            fetch_weights(weights_hbm, weights, weight_sems, part).start()

    span = 3 * WIDTH
    ready = pltpu.make_async_copy(
        early.at[slot],
        out_hbm.at[:, pl.ds(pl.multiple_of(step * span, span), 2 * WIDTH)],
        sems.at[slot],
    )
    swept = pltpu.make_async_copy(
        last.at[slot],
        out_hbm.at[:, pl.ds(pl.multiple_of(step * span + 2 * WIDTH, WIDTH), WIDTH)],
        sems.at[2 + slot],
    )
    ready_before = pltpu.make_async_copy(
        early.at[before], out_hbm.at[:, pl.ds(0, 2 * WIDTH)], sems.at[before]
    )
    swept_before = pltpu.make_async_copy(
        last.at[before], out_hbm.at[:, pl.ds(0, WIDTH)], sems.at[2 + before]
    )

    last[slot] = advance(ops_ref, state_ref[...], coef_ref[...])

    @pl.when(backward)
    def _():
        arrival.wait()
        backward_lists(arrived, weights_hbm, weights, terms, spread, wide, weight_sems)

    @pl.when(step == 0)
    def _():
        @pl.when(section_ref[0] == 1)
        def _():
            arrival.wait()
            terms[...] = arrived[...]

        sum_terms(key_ref, table_ref, terms, forcing)

    write = write_ref[...]
    coarse = write.astype(BF16).astype(F32)
    fine = write - coarse
    factor = jnp.concatenate([coarse, coarse, fine, fine], 0).astype(BF16)

    def added(start, width):
        base = step * (span // LANES) + start // LANES
        fields = jnp.concatenate(
            [
                forcing[pl.ds(pl.multiple_of((base + t) * 8, 8), 8), :]
                for t in range(width // LANES)
            ],
            1,
        )
        operand = jnp.concatenate([fields, fields], 0).astype(BF16)
        return lax.dot_general(
            factor, operand, (((0,), (0,)), ((), ())), preferred_element_type=F32
        )

    fetch(step, slot).wait()
    early[slot] = (early[slot].astype(F32) + added(0, 2 * WIDTH)).astype(BF16)
    ready.start()
    last[slot] = (last[slot].astype(F32) + added(2 * WIDTH, WIDTH)).astype(BF16)
    swept.start()

    @pl.when(step > 0)
    def _():
        ready_before.wait()
        swept_before.wait()

    @pl.when(step < pl.num_programs(0) - 1)
    def _():
        fetch(step + 1, before).start()

    @pl.when(step == pl.num_programs(0) - 1)
    def _():
        ready.wait()
        swept.wait()


def late(section, key, table, arrived, weights, write, ops, swept, state, coef):
    levels, cells = state.shape
    slots, width = arrived.shape
    whole = pl.BlockSpec(memory_space=pltpu.VMEM)
    columns = pl.BlockSpec((levels, WIDTH), lambda i: (0, 3 * i + 2))
    return pl.pallas_call(
        late_kernel,
        grid=(cells // (3 * WIDTH),),
        out_shape=jax.ShapeDtypeStruct((levels, cells), BF16),
        in_specs=[
            pl.BlockSpec(memory_space=pltpu.SMEM),
            whole,
            whole,
            pl.BlockSpec(memory_space=pl.ANY),
            pl.BlockSpec(memory_space=pl.ANY),
            whole,
            whole,
            pl.BlockSpec(memory_space=pl.ANY),
            columns,
            columns,
        ],
        out_specs=pl.BlockSpec(memory_space=pl.ANY),
        scratch_shapes=[
            pltpu.VMEM((slots, width), BF16),
            pltpu.VMEM((slots, width), BF16),
            pltpu.VMEM((cells // LANES * 8, LANES), F32),
            pltpu.VMEM((2, levels, 2 * WIDTH), BF16),
            pltpu.VMEM((2, levels, WIDTH), BF16),
            pltpu.VMEM((LANES, 8 * LANES), BF16),
            pltpu.VMEM((MANY * LANES, 16 * LANES), F32),
            pltpu.VMEM(weights.shape, BF16),
            pltpu.SemaphoreType.DMA((weights.shape[0] // GROUP,)),
            pltpu.SemaphoreType.DMA((7,)),
        ],
        compiler_params=pltpu.CompilerParams(vmem_limit_bytes=36 << 20),
        name="late",
    )(section, key, table, arrived, weights, write, ops, swept, state, coef)


def body(
    adjoint_state,
    tangent_coef,
    column_ops,
    surf_read,
    surf_write,
    remap_weights,
    pair_atmos,
    pair_ocean,
    list_len,
    ocean_owned,
):
    section = lax.axis_index("sec")
    lists, cap = pair_atmos.shape[1:]
    state = pltpu.with_memory_space_constraint(adjoint_state[0], pltpu.HBM)
    coef = pltpu.with_memory_space_constraint(tangent_coef[0], pltpu.HBM)
    weights = pltpu.with_memory_space_constraint(
        remap_weights[0].reshape(lists, cap // 8, 8, BLK * BLK), pltpu.HBM
    )
    ops = column_ops[0]
    which = section.reshape(1).astype(jnp.int32)
    arrived_ids = lax.all_to_all(pair_ocean[0], "tile", split_axis=0, concat_axis=0, tiled=True)
    read = pltpu.with_memory_space_constraint(surf_read[0], pltpu.HBM)
    surface, swept = surface_blocks(read, ops, state, coef)
    partner = lax.ppermute(surface, "sec", [(0, 1), (1, 0)])
    payload, in_key, in_table = outgoing(
        which,
        pair_atmos[0].T,
        list_len,
        arrived_ids.reshape(lists, 1, cap),
        ocean_owned,
        partner,
        weights,
    )
    received = lax.all_to_all(
        payload.reshape(lists, cap, NF * BLK), "tile", split_axis=0, concat_axis=0, tiled=True
    )
    swept = early_sweep(ops, state, coef, swept, FIRST, 6)
    swept = pltpu.with_memory_space_constraint(swept, pltpu.HBM)
    arrived = received.reshape(lists * cap, NF * BLK)
    write = surf_write[0].T
    out = late(which, in_key, in_table, arrived, weights, write, ops, swept, state, coef)
    return out[None]


def solution(mesh):
    in_specs = (
        P("sec", None, "tile"),
        P("sec", None, "tile"),
        P("sec", None, None, None),
        P("sec", None, None),
        P("sec", None, None),
        P("tile", None, None, None),
        P("tile", None, None),
        P("tile", None, None),
        P("tile", None),
        P("tile", None),
    )
    out_specs = P("sec", None, "tile")
    return jax.shard_map(body, mesh=mesh, in_specs=in_specs, out_specs=out_specs, check_vma=False)
```

profile of v0, /device:TPU:1, one launch (start us, length us, event | category | flops | bytes accessed | tf_op | source)
XLA Modules:
  0.0 72.6 jit_solution(8271541936000403753)
XLA Ops:
  0.0 1.0 %copy.15 = bf16[1,16,75,75]{3,2,1,0:T(8,128)(2,1)S(1)} copy(bf16[1,16,75,75]{3,1,2,0:T(8,128)(2,1)} %param.12) | data formatting | bytes 360000 | tf_op args[2]
  1.1 0.0 copy-start.4
  1.1 0.0 copy-start
  1.1 0.0 copy-start.1
  1.1 0.0 copy-start.3
  1.1 10.1 %surface.1 = (bf16[576,256]{1,0:T(8,128)(2,1)S(1)}, bf16[75,24576]{1,0:T(8,128)(2,1)}) custom-call(bf16[4,75]{1,0:T(4,128)(2,1)} %bitcast.32, bf16[16,75,75]{2,1,0:T(8,128)(2,1)S(1)} %bitcast.18, bf16[75,36864]{1,0:T(8,128)(2,1)} %bitcast.24, bf16[75,36864]{1,0:T(8,128)(2,1)} %bitcast.27), custom_call_target="tpu_custom_call" | custom-call | tf_op jit(solution)/shard_map/surface/pallas_call | solution.py:112
  11.2 1.5 %collective-permute-start = (bf16[576,256]{1,0:T(8,128)(2,1)S(1)}, bf16[576,256]{1,0:T(8,128)(2,1)S(1)}, u32[]{:S(2)}, u32[]{:S(2)}) collective-permute-start(bf16[576,256]{1,0:T(8,128)(2,1)S(1)} %get-tuple-element.10), channel_id=1, source_target_pairs={{0,64},{64,0},{1,65},{65,1},{2,66},{66,2},{3,67},{67,3},{4,68},{68... | collective-permute-start | bytes 884744 | tf_op jit(solution)/shard_map/ppermute | solution.py:605
  12.6 0.0 copy-done.4
  12.6 0.7 copy.12
  13.3 11.2 %all-to-all-start = ((s32[64,1,16]{2,1,0:T(1,128)}), s32[64,1,16]{2,1,0:T(1,128)S(1)}, u32[]{:S(2)}, u32[]{:S(2)}) async-start(s32[64,1,16]{2,1,0:T(1,128)} %bitcast.3), calls=%async_computation | async-start | bytes 65536 | tf_op jit(solution)/shard_map/all_to_all | solution.py:602
  24.6 8.3 %all-to-all-done.ids_ref = s32[64,1,16]{2,1,0:T(1,128)S(1)} async-done(((s32[64,1,16]{2,1,0:T(1,128)}), s32[64,1,16]{2,1,0:T(1,128)S(1)}, u32[]{:S(2)}, u32[]{:S(2)}) %all-to-all-start) | async-done | bytes 4128 | tf_op jit(solution)/shard_map/all_to_all | solution.py:602
  32.9 0.0 collective-permute-done.blocks_ref
  32.9 0.0 copy-done
  32.9 0.0 copy-done.1
  32.9 0.0 copy-done.3
  32.9 6.4 %outgoing.1 = (bf16[1024,256]{1,0:T(8,128)(2,1)}, f32[8,128]{1,0:T(8,128)S(1)}, f32[1,640]{1,0:T(1,128)S(1)}) custom-call(s32[1]{0:T(128)} %bitcast.section_ref, s32[16,64]{1,0:T(8,128)S(1)} %bitcast.22, s32[1,64]{1,0:T(1,128)S(1)} %copy-done.3, s32[64,1,16]{2,1,0:T(1,128)S(1)} %all-to-all-done.ids_ref, s32[1,576]{1,0:T(1,128)S(1)} %copy-done.1, ...), custom_call_target="tpu_custom_call" | custom-call | tf_op jit(solution)/shard_map/outgoing/pallas_call | solution.py:314
  39.4 4.9 %all-to-all-start.1 = ((bf16[64,16,256]{2,1,0:T(8,128)(2,1)}), bf16[64,16,256]{2,1,0:T(8,128)(2,1)S(1)}, u32[]{:S(2)}, u32[]{:S(2)}) async-start(bf16[64,16,256]{2,1,0:T(8,128)(2,1)} %bitcast.9), calls=%async_computation.1 | async-start | bytes 1048576 | tf_op jit(solution)/shard_map/all_to_all | solution.py:615
  44.3 0.0 copy-start.2
  44.3 14.0 %early.1.swept_hbm = bf16[75,24576]{1,0:T(8,128)(2,1)} custom-call(bf16[16,75,75]{2,1,0:T(8,128)(2,1)S(1)} %bitcast.19, bf16[75,36864]{1,0:T(8,128)(2,1)} %bitcast.25, bf16[75,36864]{1,0:T(8,128)(2,1)} %bitcast.28, bf16[75,24576]{1,0:T(8,128)(2,1)} %get-tuple-element.14.swept_hbm), custom_call_target="tpu_custom_call", output_to_operand_aliasing={{}: (3, {})} | custom-call | tf_op jit(solution)/shard_map/early/pallas_call | solution.py:343
  58.2 0.0 all-to-all-done.1
  58.2 0.0 copy-done.2
  58.2 14.2 %late.1 = bf16[75,36864]{1,0:T(8,128)(2,1)} custom-call(s32[1]{0:T(128)} %bitcast.section_ref, f32[8,128]{1,0:T(8,128)S(1)} %get-tuple-element.11.key_ref, f32[1,640]{1,0:T(1,128)S(1)} %get-tuple-element.12.table_ref, bf16[1024,256]{1,0:T(8,128)(2,1)S(1)} %bitcast.21, bf16[64,2,8,4096]{3,2,1,0:T(8,128)(2,1)} %bitcast.31, f32[4,75]{1,0:T(4,128)S(1)} %bitcast.23, ...), custom_call_target="tpu_custom_call" | custom-call | tf_op jit(solution)/shard_map/late/pallas_call | solution.py:547
Async XLA Ops:
  1.1 11.6 %copy-start.4 = (s32[1,64,16]{1,2,0:T(8,128)S(1)}, s32[1,64,16]{1,2,0:T(8,128)}, u32[]{:S(2)}) copy-start(s32[1,64,16]{1,2,0:T(8,128)} %param.17) | copy-start | bytes 12292
  1.1 31.9 %copy-start = (s32[1,64,16]{1,2,0:T(8,128)S(1)}, s32[1,64,16]{1,2,0:T(8,128)}, u32[]{:S(2)}) copy-start(s32[1,64,16]{1,2,0:T(8,128)} %param.16) | copy-start | bytes 12292
  1.1 31.9 %copy-start.1 = (s32[1,576]{1,0:T(1,128)S(1)}, s32[1,576]{1,0:T(1,128)}, u32[]{:S(2)}) copy-start(s32[1,576]{1,0:T(1,128)} %owned_ref.1) | copy-start | bytes 6916
  1.1 31.8 %copy-start.3 = (s32[1,64]{1,0:T(1,128)S(1)}, s32[1,64]{1,0:T(1,128)}, u32[]{:S(2)}) copy-start(s32[1,64]{1,0:T(1,128)} %length_ref.1) | copy-start | bytes 772
  11.2 21.8 %collective-permute-start = (bf16[576,256]{1,0:T(8,128)(2,1)S(1)}, bf16[576,256]{1,0:T(8,128)(2,1)S(1)}, u32[]{:S(2)}, u32[]{:S(2)}) collective-permute-start(bf16[576,256]{1,0:T(8,128)(2,1)S(1)} %get-tuple-element.10), channel_id=1, source_target_pairs={{0,64},{64,0},{1,65},{65,1},{2,66},{66,2},{3,67},{67,3},{4,68},{68... | collective-permute-start | bytes 884744 | tf_op jit(solution)/shard_map/ppermute | solution.py:605
  13.3 19.6 %all-to-all-start = ((s32[64,1,16]{2,1,0:T(1,128)}), s32[64,1,16]{2,1,0:T(1,128)S(1)}, u32[]{:S(2)}, u32[]{:S(2)}) async-start(s32[64,1,16]{2,1,0:T(1,128)} %bitcast.3), calls=%async_computation | async-start | bytes 65536 | tf_op jit(solution)/shard_map/all_to_all | solution.py:602
  39.4 18.9 %all-to-all-start.1 = ((bf16[64,16,256]{2,1,0:T(8,128)(2,1)}), bf16[64,16,256]{2,1,0:T(8,128)(2,1)S(1)}, u32[]{:S(2)}, u32[]{:S(2)}) async-start(bf16[64,16,256]{2,1,0:T(8,128)(2,1)} %bitcast.9), calls=%async_computation.1 | async-start | bytes 1048576 | tf_op jit(solution)/shard_map/all_to_all | solution.py:615
  44.3 14.0 %copy-start.2 = (f32[1,75,4]{1,2,0:T(4,128)S(1)}, f32[1,75,4]{1,2,0:T(4,128)}, u32[]{:S(2)}) copy-start(f32[1,75,4]{1,2,0:T(4,128)} %param.14) | copy-start | bytes 3604
where the time goes:
time: 73.5 us; the launch traced here: 72.6 us
  Pallas kernels  44.6 us (61%)
  starting transfers between devices  17.6 us (24%)
  waiting for transfers between devices  8.35 us (11%)
  local copies, waits for them, and re-layouts  1.78 us (2%)
    pallas_call x1, Pallas kernels, late(): pl.pallas_call(late_kernel, grid=(cells // (3 * WIDTH),), out_shape=jax.S...  14.2 us
    pallas_call x1, Pallas kernels, early_sweep(): pl.pallas_call(early_kernel, grid=(stop - start,), out_shape=pltpu.HBM(sw...  14 us
    all_to_all x1, starting transfers between devices, body(): lax.all_to_all(pair_ocean[0], 'tile', split_axis=0, concat_axis=0, tiled=...  11.2 us
    pallas_call x1, Pallas kernels, surface_blocks(): pl.pallas_call(surface_kernel, out_shape=(jax.ShapeDtypeStruct((blocks, N...  10.1 us
    all_to_all x1, waiting for transfers between devices, body(): lax.all_to_all(pair_ocean[0], 'tile', split_axis=0, concat_axis=0, tiled=...  8.35 us
    pallas_call x1, Pallas kernels, outgoing(): pl.pallas_call(outgoing_kernel, out_shape=(jax.ShapeDtypeStruct((slots, w...  6.42 us
    all_to_all x1, starting transfers between devices, body(): lax.all_to_all(payload.reshape(lists, cap, NF * BLK), 'tile', split_axis=...  4.88 us
    unnamed x12, local copies, waits for them, and re-layouts  1.78 us
  transfers between devices with their start and end apart: 3, of which 1 were waited for; matrix products, arithmetic and copies ran while one was open for 1% of the time, Pallas kernels for 19%

commit v1 on v0

--- a/solution.py
+++ b/solution.py
@@ -36,10 +36,24 @@
 
 
 def surface_kernel(
-    read_ref, ops_ref, state_hbm, coef_hbm, out_ref, swept_hbm, state, coef, swept, held, sems
+    read_ref,
+    given_hbm,
+    state_hbm,
+    coef_hbm,
+    out_ref,
+    swept_hbm,
+    ops_ref,
+    given,
+    state,
+    coef,
+    swept,
+    held,
+    sems,
 ):
     count = coef.shape[0]
-    parts = sems.shape[0] - 2 * count
+    parts = sems.shape[0] - 2 * count - 1
+    operators = pltpu.make_async_copy(given_hbm, given, sems.at[parts + 2 * count])
+    operators.start()
     tiles = WIDTH // LANES
 
     def columns(part):
@@ -67,6 +81,9 @@
     for part in range(parts):
         if part not in ahead:
             fetch(part).start()
+
+    operators.wait()
+    ops_ref[...] = jnp.swapaxes(given[...].astype(F32), 0, 1).astype(BF16)
 
     def sweep_block(block, carry):
         part = early_column(block)
@@ -103,7 +120,7 @@
         store(block).wait()
 
 
-def surface_blocks(read, ops, state, coef):
+def surface_blocks(read, given, state, coef):
     levels, cells = state.shape
     blocks = cells // BLK
     parts = cells // WIDTH
@@ -114,19 +131,21 @@
         out_shape=(
             jax.ShapeDtypeStruct((blocks, NF * BLK), BF16),
             pltpu.HBM((levels, cells // 3 * 2), BF16),
+            jax.ShapeDtypeStruct((NSTEP, levels, levels), BF16),
         ),
-        in_specs=[whole, whole, there, there],
-        out_specs=(whole, there),
+        in_specs=[whole, there, there, there],
+        out_specs=(whole, there, whole),
         scratch_shapes=[
+            pltpu.VMEM(given.shape, BF16),
             pltpu.VMEM((levels, cells), BF16),
             pltpu.VMEM((FIRST, levels, WIDTH), BF16),
             pltpu.VMEM((FIRST, levels, WIDTH), BF16),
             pltpu.VMEM((blocks // 2 * 8, LANES), F32),
-            pltpu.SemaphoreType.DMA((parts + 2 * FIRST,)),
+            pltpu.SemaphoreType.DMA((parts + 2 * FIRST + 1,)),
         ],
         compiler_params=pltpu.CompilerParams(vmem_limit_bytes=28 << 20),
         name="surface",
-    )(read, ops, state, coef)
+    )(read, given, state, coef)
 
 
 def fetch_weights(weights_hbm, weights, sems, part):
@@ -597,11 +616,11 @@
     weights = pltpu.with_memory_space_constraint(
         remap_weights[0].reshape(lists, cap // 8, 8, BLK * BLK), pltpu.HBM
     )
-    ops = column_ops[0]
+    given = pltpu.with_memory_space_constraint(column_ops[0].transpose(1, 0, 2), pltpu.HBM)
     which = section.reshape(1).astype(jnp.int32)
     arrived_ids = lax.all_to_all(pair_ocean[0], "tile", split_axis=0, concat_axis=0, tiled=True)
     read = pltpu.with_memory_space_constraint(surf_read[0], pltpu.HBM)
-    surface, swept = surface_blocks(read, ops, state, coef)
+    surface, swept, ops = surface_blocks(read, given, state, coef)
     partner = lax.ppermute(surface, "sec", [(0, 1), (1, 0)])
     payload, in_key, in_table = outgoing(
         which,

time: 73.5 us -> 72.6 us (0.988)
  local copies, waits for them, and re-layouts: 1.78 us -> 0.72 us
    unnamed x12 -> x11, local copies, waits for them, and re-layouts: 1.78 us -> 0.72 us
  transfers between devices with their start and end apart: 3 -> 3, of which waited for: 1 -> 1; matrix products, arithmetic and copies ran while one was open for 1% -> 1% of each run, Pallas kernels for 19% -> 20%
where the time goes in v1:
time: 72.6 us; the launch traced here: 71.6 us
  Pallas kernels  44.7 us (62%)
  starting transfers between devices  17.6 us (24%)
  waiting for transfers between devices  8.35 us (12%)
    pallas_call x1, Pallas kernels, late(): pl.pallas_call(late_kernel, grid=(cells // (3 * WIDTH),), out_shape=jax.S...  14.2 us
    pallas_call x1, Pallas kernels, early_sweep(): pl.pallas_call(early_kernel, grid=(stop - start,), out_shape=pltpu.HBM(sw...  14 us
    all_to_all x1, starting transfers between devices, body(): lax.all_to_all(pair_ocean[0], 'tile', split_axis=0, concat_axis=0, tiled=...  11.2 us
    pallas_call x1, Pallas kernels, surface_blocks(): pl.pallas_call(surface_kernel, out_shape=(jax.ShapeDtypeStruct((blocks, N...  10.2 us
    all_to_all x1, waiting for transfers between devices, body(): lax.all_to_all(pair_ocean[0], 'tile', split_axis=0, concat_axis=0, tiled=...  8.35 us
    pallas_call x1, Pallas kernels, outgoing(): pl.pallas_call(outgoing_kernel, out_shape=(jax.ShapeDtypeStruct((slots, w...  6.42 us
    all_to_all x1, starting transfers between devices, body(): lax.all_to_all(payload.reshape(lists, cap, NF * BLK), 'tile', split_axis=...  4.88 us
    ppermute x1, starting transfers between devices, body(): partner = lax.ppermute(surface, 'sec', [(0, 1), (1, 0)])  1.46 us
  transfers between devices with their start and end apart: 3, of which 1 were waited for; matrix products, arithmetic and copies ran while one was open for 1% of the time, Pallas kernels for 20%

profile of v1, /device:TPU:1, one launch (start us, length us, event | category | flops | bytes accessed | tf_op | source)
XLA Modules:
  0.0 71.6 jit_solution(14567711123893098969)
XLA Ops:
  0.0 0.0 copy-start.4
  0.0 0.0 copy-start
  0.0 0.0 copy-start.1
  0.0 0.0 copy-start.3
  0.0 10.2 %surface.1 = (bf16[576,256]{1,0:T(8,128)(2,1)S(1)}, bf16[75,24576]{1,0:T(8,128)(2,1)}, bf16[16,75,75]{2,1,0:T(8,128)(2,1)S(1)}) custom-call(bf16[4,75]{1,0:T(4,128)(2,1)} %bitcast.30, bf16[75,16,75]{2,1,0:T(8,128)(2,1)} %bitcast.29, bf16[75,36864]{1,0:T(8,128)(2,1)} %bitcast.21, bf16[75,36864]{1,0:T(8,128)(2,1)} %bitcast.24), custom_call_target="tpu_custom_call" | custom-call | tf_op jit(solution)/shard_map/surface/pallas_call | solution.py:129
  10.2 1.5 %collective-permute-start = (bf16[576,256]{1,0:T(8,128)(2,1)S(1)}, bf16[576,256]{1,0:T(8,128)(2,1)S(1)}, u32[]{:S(2)}, u32[]{:S(2)}) collective-permute-start(bf16[576,256]{1,0:T(8,128)(2,1)S(1)} %get-tuple-element.11), channel_id=1, source_target_pairs={{0,64},{64,0},{1,65},{65,1},{2,66},{66,2},{3,67},{67,3},{4,68},{68... | collective-permute-start | bytes 884744 | tf_op jit(solution)/shard_map/ppermute | solution.py:624
  11.7 0.0 copy-done.4
  11.7 0.7 copy.12
  12.4 11.2 %all-to-all-start = ((s32[64,1,16]{2,1,0:T(1,128)}), s32[64,1,16]{2,1,0:T(1,128)S(1)}, u32[]{:S(2)}, u32[]{:S(2)}) async-start(s32[64,1,16]{2,1,0:T(1,128)} %bitcast.3), calls=%async_computation | async-start | bytes 65536 | tf_op jit(solution)/shard_map/all_to_all | solution.py:621
  23.6 8.3 %all-to-all-done.ids_ref = s32[64,1,16]{2,1,0:T(1,128)S(1)} async-done(((s32[64,1,16]{2,1,0:T(1,128)}), s32[64,1,16]{2,1,0:T(1,128)S(1)}, u32[]{:S(2)}, u32[]{:S(2)}) %all-to-all-start) | async-done | bytes 4128 | tf_op jit(solution)/shard_map/all_to_all | solution.py:621
  32.0 0.0 collective-permute-done.blocks_ref
  32.0 0.0 copy-done
  32.0 0.0 copy-done.1
  32.0 0.0 copy-done.3
  32.0 6.4 %outgoing.1 = (bf16[1024,256]{1,0:T(8,128)(2,1)}, f32[8,128]{1,0:T(8,128)S(1)}, f32[1,640]{1,0:T(1,128)S(1)}) custom-call(s32[1]{0:T(128)} %bitcast.section_ref, s32[16,64]{1,0:T(8,128)S(1)} %bitcast.19, s32[1,64]{1,0:T(1,128)S(1)} %copy-done.3, s32[64,1,16]{2,1,0:T(1,128)S(1)} %all-to-all-done.ids_ref, s32[1,576]{1,0:T(1,128)S(1)} %copy-done.1, ...), custom_call_target="tpu_custom_call" | custom-call | tf_op jit(solution)/shard_map/outgoing/pallas_call | solution.py:333
  38.4 4.9 %all-to-all-start.1 = ((bf16[64,16,256]{2,1,0:T(8,128)(2,1)}), bf16[64,16,256]{2,1,0:T(8,128)(2,1)S(1)}, u32[]{:S(2)}, u32[]{:S(2)}) async-start(bf16[64,16,256]{2,1,0:T(8,128)(2,1)} %bitcast.10), calls=%async_computation.1 | async-start | bytes 1048576 | tf_op jit(solution)/shard_map/all_to_all | solution.py:634
  43.3 0.0 copy-start.2
  43.3 14.0 %early.1.swept_hbm = bf16[75,24576]{1,0:T(8,128)(2,1)} custom-call(bf16[16,75,75]{2,1,0:T(8,128)(2,1)S(1)} %get-tuple-element.15.ops_ref, bf16[75,36864]{1,0:T(8,128)(2,1)} %bitcast.22, bf16[75,36864]{1,0:T(8,128)(2,1)} %bitcast.25, bf16[75,24576]{1,0:T(8,128)(2,1)} %get-tuple-element.16.swept_hbm), custom_call_target="tpu_custom_call", output_to_operand_aliasing={{}: (3, {})} | custom-call | tf_op jit(solution)/shard_map/early/pallas_call | solution.py:362
  57.3 0.0 all-to-all-done.1
  57.3 0.0 copy-done.2
  57.3 14.2 %late.1 = bf16[75,36864]{1,0:T(8,128)(2,1)} custom-call(s32[1]{0:T(128)} %bitcast.section_ref, f32[8,128]{1,0:T(8,128)S(1)} %get-tuple-element.12.key_ref, f32[1,640]{1,0:T(1,128)S(1)} %get-tuple-element.13.table_ref, bf16[1024,256]{1,0:T(8,128)(2,1)S(1)} %bitcast.18, bf16[64,2,8,4096]{3,2,1,0:T(8,128)(2,1)} %bitcast.28, f32[4,75]{1,0:T(4,128)S(1)} %bitcast.20, ...), custom_call_target="tpu_custom_call" | custom-call | tf_op jit(solution)/shard_map/late/pallas_call | solution.py:566
Async XLA Ops:
  0.0 11.7 %copy-start.4 = (s32[1,64,16]{1,2,0:T(8,128)S(1)}, s32[1,64,16]{1,2,0:T(8,128)}, u32[]{:S(2)}) copy-start(s32[1,64,16]{1,2,0:T(8,128)} %param.17) | copy-start | bytes 12292
  0.0 32.0 %copy-start = (s32[1,64,16]{1,2,0:T(8,128)S(1)}, s32[1,64,16]{1,2,0:T(8,128)}, u32[]{:S(2)}) copy-start(s32[1,64,16]{1,2,0:T(8,128)} %param.16) | copy-start | bytes 12292
  0.0 32.0 %copy-start.1 = (s32[1,576]{1,0:T(1,128)S(1)}, s32[1,576]{1,0:T(1,128)}, u32[]{:S(2)}) copy-start(s32[1,576]{1,0:T(1,128)} %owned_ref.1) | copy-start | bytes 6916
  0.0 32.0 %copy-start.3 = (s32[1,64]{1,0:T(1,128)S(1)}, s32[1,64]{1,0:T(1,128)}, u32[]{:S(2)}) copy-start(s32[1,64]{1,0:T(1,128)} %length_ref.1) | copy-start | bytes 772
  10.2 21.8 %collective-permute-start = (bf16[576,256]{1,0:T(8,128)(2,1)S(1)}, bf16[576,256]{1,0:T(8,128)(2,1)S(1)}, u32[]{:S(2)}, u32[]{:S(2)}) collective-permute-start(bf16[576,256]{1,0:T(8,128)(2,1)S(1)} %get-tuple-element.11), channel_id=1, source_target_pairs={{0,64},{64,0},{1,65},{65,1},{2,66},{66,2},{3,67},{67,3},{4,68},{68... | collective-permute-start | bytes 884744 | tf_op jit(solution)/shard_map/ppermute | solution.py:624
  12.4 19.6 %all-to-all-start = ((s32[64,1,16]{2,1,0:T(1,128)}), s32[64,1,16]{2,1,0:T(1,128)S(1)}, u32[]{:S(2)}, u32[]{:S(2)}) async-start(s32[64,1,16]{2,1,0:T(1,128)} %bitcast.3), calls=%async_computation | async-start | bytes 65536 | tf_op jit(solution)/shard_map/all_to_all | solution.py:621
  38.4 18.9 %all-to-all-start.1 = ((bf16[64,16,256]{2,1,0:T(8,128)(2,1)}), bf16[64,16,256]{2,1,0:T(8,128)(2,1)S(1)}, u32[]{:S(2)}, u32[]{:S(2)}) async-start(bf16[64,16,256]{2,1,0:T(8,128)(2,1)} %bitcast.10), calls=%async_computation.1 | async-start | bytes 1048576 | tf_op jit(solution)/shard_map/all_to_all | solution.py:634
  43.3 14.0 %copy-start.2 = (f32[1,75,4]{1,2,0:T(4,128)S(1)}, f32[1,75,4]{1,2,0:T(4,128)}, u32[]{:S(2)}) copy-start(f32[1,75,4]{1,2,0:T(4,128)} %param.14) | copy-start | bytes 3604

commit v2 on v1

--- a/solution.py
+++ b/solution.py
@@ -10,7 +10,7 @@
 NSTEP = 16
 LANES = 128
 GROUP = 8
-MANY = 2
+MANY = 4
 WIDTH = 4096
 FIRST = 2
 BF16 = jnp.bfloat16
@@ -36,13 +36,14 @@
 
 
 def surface_kernel(
-    read_ref,
+    read_hbm,
     given_hbm,
     state_hbm,
     coef_hbm,
     out_ref,
     swept_hbm,
     ops_ref,
+    read_ref,
     given,
     state,
     coef,
@@ -51,9 +52,11 @@
     sems,
 ):
     count = coef.shape[0]
-    parts = sems.shape[0] - 2 * count - 1
+    parts = sems.shape[0] - 2 * count - 2
+    reading = pltpu.make_async_copy(read_hbm, read_ref, sems.at[parts + 2 * count + 1])
     operators = pltpu.make_async_copy(given_hbm, given, sems.at[parts + 2 * count])
     operators.start()
+    reading.start()
     tiles = WIDTH // LANES
 
     def columns(part):
@@ -83,6 +86,7 @@
             fetch(part).start()
 
     operators.wait()
+    reading.wait()
     ops_ref[...] = jnp.swapaxes(given[...].astype(F32), 0, 1).astype(BF16)
 
     def sweep_block(block, carry):
@@ -133,15 +137,16 @@
             pltpu.HBM((levels, cells // 3 * 2), BF16),
             jax.ShapeDtypeStruct((NSTEP, levels, levels), BF16),
         ),
-        in_specs=[whole, there, there, there],
+        in_specs=[there] * 4,
         out_specs=(whole, there, whole),
         scratch_shapes=[
+            pltpu.VMEM(read.shape, BF16),
             pltpu.VMEM(given.shape, BF16),
             pltpu.VMEM((levels, cells), BF16),
             pltpu.VMEM((FIRST, levels, WIDTH), BF16),
             pltpu.VMEM((FIRST, levels, WIDTH), BF16),
             pltpu.VMEM((blocks // 2 * 8, LANES), F32),
-            pltpu.SemaphoreType.DMA((parts + 2 * FIRST + 1,)),
+            pltpu.SemaphoreType.DMA((parts + 2 * FIRST + 2,)),
         ],
         compiler_params=pltpu.CompilerParams(vmem_limit_bytes=28 << 20),
         name="surface",

time: 72.6 us -> 71.4 us (0.983)
  Pallas kernels: 44.7 us -> 43.7 us
where the time goes in v2:
time: 71.4 us; the launch traced here: 70.6 us
  Pallas kernels  43.7 us (61%)
  starting transfers between devices  17.6 us (25%)
  waiting for transfers between devices  8.35 us (12%)
  local copies, waits for them, and re-layouts  0.72 us (1%)
    pallas_call x1, Pallas kernels, late(): pl.pallas_call(late_kernel, grid=(cells // (3 * WIDTH),), out_shape=jax.S...  14.2 us
    pallas_call x1, Pallas kernels, early_sweep(): pl.pallas_call(early_kernel, grid=(stop - start,), out_shape=pltpu.HBM(sw...  14 us
    all_to_all x1, starting transfers between devices, body(): lax.all_to_all(pair_ocean[0], 'tile', split_axis=0, concat_axis=0, tiled=...  11.2 us
    pallas_call x1, Pallas kernels, surface_blocks(): pl.pallas_call(surface_kernel, out_shape=(jax.ShapeDtypeStruct((blocks, N...  9.52 us
    all_to_all x1, waiting for transfers between devices, body(): lax.all_to_all(pair_ocean[0], 'tile', split_axis=0, concat_axis=0, tiled=...  8.35 us
    pallas_call x1, Pallas kernels, outgoing(): pl.pallas_call(outgoing_kernel, out_shape=(jax.ShapeDtypeStruct((slots, w...  6.08 us
    all_to_all x1, starting transfers between devices, body(): lax.all_to_all(payload.reshape(lists, cap, NF * BLK), 'tile', split_axis=...  4.87 us
    ppermute x1, starting transfers between devices, body(): partner = lax.ppermute(surface, 'sec', [(0, 1), (1, 0)])  1.46 us
  transfers between devices with their start and end apart: 3, of which 1 were waited for; matrix products, arithmetic and copies ran while one was open for 1% of the time, Pallas kernels for 20%

profile of v2, /device:TPU:1, one launch (start us, length us, event | category | flops | bytes accessed | tf_op | source)
XLA Modules:
  0.0 70.6 jit_solution(16795689239576089680)
XLA Ops:
  0.0 0.0 copy-start.4
  0.0 0.0 copy-start
  0.0 0.0 copy-start.1
  0.0 0.0 copy-start.3
  0.0 9.5 %surface.1 = (bf16[576,256]{1,0:T(8,128)(2,1)S(1)}, bf16[75,24576]{1,0:T(8,128)(2,1)}, bf16[16,75,75]{2,1,0:T(8,128)(2,1)S(1)}) custom-call(bf16[4,75]{1,0:T(4,128)(2,1)} %bitcast.30, bf16[75,16,75]{2,1,0:T(8,128)(2,1)} %bitcast.29, bf16[75,36864]{1,0:T(8,128)(2,1)} %bitcast.21, bf16[75,36864]{1,0:T(8,128)(2,1)} %bitcast.24), custom_call_target="tpu_custom_call" | custom-call | tf_op jit(solution)/shard_map/surface/pallas_call | solution.py:133
  9.6 1.5 %collective-permute-start = (bf16[576,256]{1,0:T(8,128)(2,1)S(1)}, bf16[576,256]{1,0:T(8,128)(2,1)S(1)}, u32[]{:S(2)}, u32[]{:S(2)}) collective-permute-start(bf16[576,256]{1,0:T(8,128)(2,1)S(1)} %get-tuple-element.11), channel_id=1, source_target_pairs={{0,64},{64,0},{1,65},{65,1},{2,66},{66,2},{3,67},{67,3},{4,68},{68... | collective-permute-start | bytes 884744 | tf_op jit(solution)/shard_map/ppermute | solution.py:629
  11.0 0.0 copy-done.4
  11.0 0.7 copy.12
  11.7 11.2 %all-to-all-start = ((s32[64,1,16]{2,1,0:T(1,128)}), s32[64,1,16]{2,1,0:T(1,128)S(1)}, u32[]{:S(2)}, u32[]{:S(2)}) async-start(s32[64,1,16]{2,1,0:T(1,128)} %bitcast.3), calls=%async_computation | async-start | bytes 65536 | tf_op jit(solution)/shard_map/all_to_all | solution.py:626
  23.0 8.3 %all-to-all-done.ids_ref = s32[64,1,16]{2,1,0:T(1,128)S(1)} async-done(((s32[64,1,16]{2,1,0:T(1,128)}), s32[64,1,16]{2,1,0:T(1,128)S(1)}, u32[]{:S(2)}, u32[]{:S(2)}) %all-to-all-start) | async-done | bytes 4128 | tf_op jit(solution)/shard_map/all_to_all | solution.py:626
  31.3 0.0 collective-permute-done.blocks_ref
  31.3 0.0 copy-done
  31.3 0.0 copy-done.1
  31.3 0.0 copy-done.3
  31.3 6.1 %outgoing.1 = (bf16[1024,256]{1,0:T(8,128)(2,1)}, f32[8,128]{1,0:T(8,128)S(1)}, f32[1,640]{1,0:T(1,128)S(1)}) custom-call(s32[1]{0:T(128)} %bitcast.section_ref, s32[16,64]{1,0:T(8,128)S(1)} %bitcast.19, s32[1,64]{1,0:T(1,128)S(1)} %copy-done.3, s32[64,1,16]{2,1,0:T(1,128)S(1)} %all-to-all-done.ids_ref, s32[1,576]{1,0:T(1,128)S(1)} %copy-done.1, ...), custom_call_target="tpu_custom_call" | custom-call | tf_op jit(solution)/shard_map/outgoing/pallas_call | solution.py:338
  37.4 4.9 %all-to-all-start.1 = ((bf16[64,16,256]{2,1,0:T(8,128)(2,1)}), bf16[64,16,256]{2,1,0:T(8,128)(2,1)S(1)}, u32[]{:S(2)}, u32[]{:S(2)}) async-start(bf16[64,16,256]{2,1,0:T(8,128)(2,1)} %bitcast.10), calls=%async_computation.1 | async-start | bytes 1048576 | tf_op jit(solution)/shard_map/all_to_all | solution.py:639
  42.3 0.0 copy-start.2
  42.3 14.0 %early.1.swept_hbm = bf16[75,24576]{1,0:T(8,128)(2,1)} custom-call(bf16[16,75,75]{2,1,0:T(8,128)(2,1)S(1)} %get-tuple-element.15.ops_ref, bf16[75,36864]{1,0:T(8,128)(2,1)} %bitcast.22, bf16[75,36864]{1,0:T(8,128)(2,1)} %bitcast.25, bf16[75,24576]{1,0:T(8,128)(2,1)} %get-tuple-element.16.swept_hbm), custom_call_target="tpu_custom_call", output_to_operand_aliasing={{}: (3, {})} | custom-call | tf_op jit(solution)/shard_map/early/pallas_call | solution.py:367
  56.3 0.0 all-to-all-done.1
  56.3 0.0 copy-done.2
  56.3 14.2 %late.1 = bf16[75,36864]{1,0:T(8,128)(2,1)} custom-call(s32[1]{0:T(128)} %bitcast.section_ref, f32[8,128]{1,0:T(8,128)S(1)} %get-tuple-element.12.key_ref, f32[1,640]{1,0:T(1,128)S(1)} %get-tuple-element.13.table_ref, bf16[1024,256]{1,0:T(8,128)(2,1)S(1)} %bitcast.18, bf16[64,2,8,4096]{3,2,1,0:T(8,128)(2,1)} %bitcast.28, f32[4,75]{1,0:T(4,128)S(1)} %bitcast.20, ...), custom_call_target="tpu_custom_call" | custom-call | tf_op jit(solution)/shard_map/late/pallas_call | solution.py:571
Async XLA Ops:
  0.0 11.0 %copy-start.4 = (s32[1,64,16]{1,2,0:T(8,128)S(1)}, s32[1,64,16]{1,2,0:T(8,128)}, u32[]{:S(2)}) copy-start(s32[1,64,16]{1,2,0:T(8,128)} %param.17) | copy-start | bytes 12292
  0.0 31.3 %copy-start = (s32[1,64,16]{1,2,0:T(8,128)S(1)}, s32[1,64,16]{1,2,0:T(8,128)}, u32[]{:S(2)}) copy-start(s32[1,64,16]{1,2,0:T(8,128)} %param.16) | copy-start | bytes 12292
  0.0 31.3 %copy-start.1 = (s32[1,576]{1,0:T(1,128)S(1)}, s32[1,576]{1,0:T(1,128)}, u32[]{:S(2)}) copy-start(s32[1,576]{1,0:T(1,128)} %owned_ref.1) | copy-start | bytes 6916
  0.0 31.3 %copy-start.3 = (s32[1,64]{1,0:T(1,128)S(1)}, s32[1,64]{1,0:T(1,128)}, u32[]{:S(2)}) copy-start(s32[1,64]{1,0:T(1,128)} %length_ref.1) | copy-start | bytes 772
  9.6 21.8 %collective-permute-start = (bf16[576,256]{1,0:T(8,128)(2,1)S(1)}, bf16[576,256]{1,0:T(8,128)(2,1)S(1)}, u32[]{:S(2)}, u32[]{:S(2)}) collective-permute-start(bf16[576,256]{1,0:T(8,128)(2,1)S(1)} %get-tuple-element.11), channel_id=1, source_target_pairs={{0,64},{64,0},{1,65},{65,1},{2,66},{66,2},{3,67},{67,3},{4,68},{68... | collective-permute-start | bytes 884744 | tf_op jit(solution)/shard_map/ppermute | solution.py:629
  11.7 19.6 %all-to-all-start = ((s32[64,1,16]{2,1,0:T(1,128)}), s32[64,1,16]{2,1,0:T(1,128)S(1)}, u32[]{:S(2)}, u32[]{:S(2)}) async-start(s32[64,1,16]{2,1,0:T(1,128)} %bitcast.3), calls=%async_computation | async-start | bytes 65536 | tf_op jit(solution)/shard_map/all_to_all | solution.py:626
  37.4 18.9 %all-to-all-start.1 = ((bf16[64,16,256]{2,1,0:T(8,128)(2,1)}), bf16[64,16,256]{2,1,0:T(8,128)(2,1)S(1)}, u32[]{:S(2)}, u32[]{:S(2)}) async-start(bf16[64,16,256]{2,1,0:T(8,128)(2,1)} %bitcast.10), calls=%async_computation.1 | async-start | bytes 1048576 | tf_op jit(solution)/shard_map/all_to_all | solution.py:639
  42.3 14.0 %copy-start.2 = (f32[1,75,4]{1,2,0:T(4,128)S(1)}, f32[1,75,4]{1,2,0:T(4,128)}, u32[]{:S(2)}) copy-start(f32[1,75,4]{1,2,0:T(4,128)} %param.14) | copy-start | bytes 3604
